TPU v7x, 256 devices: a whole 4x4x8 slice. The times are simulated.
256 devices in a mesh: lat: 8 (over x, core), lon: 32 (over z, y).
Axes of the slice: x: 4, y: 4, z: 8, core: 2. Of those that a mesh axis runs over, the one named last changes fastest.
Arguments:
- features: bfloat16 [256, 512, 768], P('lat', 'lon'), may hold values from -6 to 6
- cotangent: bfloat16 [256, 512, 768], P('lat', 'lon'), may hold values from -6 to 6
- weight_first: bfloat16 [2, 8, 96, 96], replicated, may hold values from -1 to 1
- weight_second: bfloat16 [2, 8, 96, 96], replicated, may hold values from -1 to 1
Outputs:
- mixed_field: bfloat16 [256, 512, 768], P('lat', 'lon')
- feature_grad: bfloat16 [256, 512, 768], P('lat', 'lon')
- grad_first: float32 [2, 8, 96, 96], replicated
- grad_second: float32 [2, 8, 96, 96], replicated
All inputs are finite; a program needn't handle non-finite values.
Results may differ from a plain program's by a relative error of at most 0.012.
The roundings to bfloat16 on the way count: a program that leaves them out, or rounds other values in their place, can miss the bound.
Values may be sent and summed in bfloat16 or wider, within the bound.
A program may use at most 64 MiB of HBM per device.

v0:
```python
import math
import jax
import jax.numpy as jnp
from jax import lax
from jax.sharding import PartitionSpec as P

NB = 8
BS = 96
KWD = 1
shrink_level = 0.01
gelu_coeff = 0.7978845608028654


def wave_table(first, second, length):
    product = first[:, None] * second[None, :] % length
    angle = 2.0 * math.pi / length * product.astype(jnp.float32)
    return (jnp.cos(angle) / math.sqrt(length), jnp.sin(angle) / math.sqrt(length))


def batch_product(left, weights):
    return jnp.einsum("mbi,bio->mbo", left, weights, preferred_element_type=jnp.float32)


def batch_back(left, weights):
    return jnp.einsum("mbo,bio->mbi", left, weights, preferred_element_type=jnp.float32)


def batch_outer(left, right):
    return jnp.einsum("mbi,mbo->bio", left, right, preferred_element_type=jnp.float32)


def gelu_parts(values):
    squared = values * values
    tangent = jnp.tanh(gelu_coeff * (values + 0.044715 * squared * values))
    result = 0.5 * values * (1.0 + tangent)
    slope = 0.5 * (1.0 + tangent) + 0.5 * values * (1.0 - tangent * tangent) * gelu_coeff * (
        1.0 + 3.0 * 0.044715 * squared
    )
    return (result, slope)


def shrink_parts(values):
    ratio = jnp.tanh(values / shrink_level)
    return (values - shrink_level * ratio, ratio * ratio)


def spectral_block(real_in, imag_in, real_cot, imag_cot, mode_weight, weight_first, weight_second):
    first_re, first_im = (weight_first[0], weight_first[1])
    second_re, second_im = (weight_second[0], weight_second[1])
    pre_real = batch_product(real_in, first_re) - batch_product(imag_in, first_im)
    pre_imag = batch_product(real_in, first_im) + batch_product(imag_in, first_re)
    act_real, slope_real = gelu_parts(pre_real)
    act_imag, slope_imag = gelu_parts(pre_imag)
    hidden_real = act_real.astype(jnp.bfloat16)
    hidden_imag = act_imag.astype(jnp.bfloat16)
    post_real = batch_product(hidden_real, second_re) - batch_product(hidden_imag, second_im)
    post_imag = batch_product(hidden_real, second_im) + batch_product(hidden_imag, second_re)
    shr_real, pass_real = shrink_parts(post_real)
    shr_imag, pass_imag = shrink_parts(post_imag)
    out_real = shr_real.astype(jnp.bfloat16)
    out_imag = shr_imag.astype(jnp.bfloat16)
    grad_post_real = (mode_weight * real_cot.astype(jnp.float32) * pass_real).astype(jnp.bfloat16)
    grad_post_imag = (mode_weight * imag_cot.astype(jnp.float32) * pass_imag).astype(jnp.bfloat16)
    grad_hid_real = batch_back(grad_post_real, second_re) + batch_back(grad_post_imag, second_im)
    grad_hid_imag = batch_back(grad_post_imag, second_re) - batch_back(grad_post_real, second_im)
    grad_pre_real = (grad_hid_real * slope_real).astype(jnp.bfloat16)
    grad_pre_imag = (grad_hid_imag * slope_imag).astype(jnp.bfloat16)
    back_real = (batch_back(grad_pre_real, first_re) + batch_back(grad_pre_imag, first_im)).astype(
        jnp.bfloat16
    )
    back_imag = (batch_back(grad_pre_imag, first_re) - batch_back(grad_pre_real, first_im)).astype(
        jnp.bfloat16
    )
    grad_second = jnp.stack(
        [
            batch_outer(hidden_real, grad_post_real) + batch_outer(hidden_imag, grad_post_imag),
            batch_outer(hidden_real, grad_post_imag) - batch_outer(hidden_imag, grad_post_real),
        ]
    )
    grad_first = jnp.stack(
        [
            batch_outer(real_in, grad_pre_real) + batch_outer(imag_in, grad_pre_imag),
            batch_outer(real_in, grad_pre_imag) - batch_outer(imag_in, grad_pre_real),
        ]
    )
    return (out_real, out_imag, back_real, back_imag, grad_first, grad_second)


def lon_transpose(source, split_dim, concat_dim):
    return lax.all_to_all(source, "lon", split_axis=split_dim, concat_axis=concat_dim, tiled=True)


def shards(features, cotangent, weight_first, weight_second):
    lat_count = lax.axis_size("lat")
    lon_count = lax.axis_size("lon")
    lat_index = lax.axis_index("lat")
    lon_index = lax.axis_index("lon")
    band_rows, band_cols, channels = features.shape
    rows_total = band_rows * lat_count
    cols_total = band_cols * lon_count
    rows_each = band_rows // lon_count
    kept_total = KWD * lat_count * lon_count
    stacked = jnp.stack([features, cotangent])
    full_rows = lon_transpose(stacked, 1, 2)
    lon_cos, lon_sin = wave_table(
        jnp.arange(kept_total, dtype=jnp.int32), jnp.arange(cols_total, dtype=jnp.int32), cols_total
    )
    lon_coeffs = jnp.concatenate([lon_cos, lon_sin]).astype(jnp.bfloat16)
    product = jnp.einsum(
        "aw,rwc->rac",
        lon_coeffs,
        full_rows.reshape(2 * rows_each, cols_total, channels),
        preferred_element_type=jnp.float32,
    )
    spectral_rows = jnp.stack([product[:, :kept_total], -product[:, kept_total:]], axis=1).astype(
        jnp.bfloat16
    )
    spectral_rows = spectral_rows.reshape(2, rows_each, 2, kept_total, channels)
    gathered = lax.all_to_all(
        lax.all_to_all(spectral_rows, "lat", split_axis=3, concat_axis=1, tiled=True),
        "lon",
        split_axis=3,
        concat_axis=1,
        tiled=True,
    )
    position = jnp.arange(rows_total, dtype=jnp.int32)
    row_of = (
        position // rows_each % lat_count * band_rows
        + position // (lat_count * rows_each) * rows_each
        + position % rows_each
    )
    lat_cos, lat_sin = wave_table(jnp.arange(rows_total, dtype=jnp.int32), row_of, rows_total)
    lat_coeffs = jnp.concatenate([lat_cos, lat_sin]).astype(jnp.bfloat16)
    product = jnp.einsum(
        "ah,shrc->sarc",
        lat_coeffs,
        gathered.reshape(2, rows_total, 2, KWD * channels),
        preferred_element_type=jnp.float32,
    )
    upper = product[:, :rows_total]
    lower = product[:, rows_total:]
    spec_real = (upper[:, :, 0] + lower[:, :, 1]).astype(jnp.bfloat16)
    spec_imag = (upper[:, :, 1] - lower[:, :, 0]).astype(jnp.bfloat16)
    modes = rows_total * KWD
    held_kw = (lat_index * lon_count + lon_index) * KWD + jnp.arange(KWD, dtype=jnp.int32)
    mode_weight = jnp.broadcast_to(
        jnp.where(held_kw == 0, 1.0, 2.0).astype(jnp.float32)[None, :], (rows_total, KWD)
    ).reshape(modes, 1, 1)
    results = spectral_block(
        spec_real[0].reshape(modes, NB, BS),
        spec_imag[0].reshape(modes, NB, BS),
        spec_real[1].reshape(modes, NB, BS),
        spec_imag[1].reshape(modes, NB, BS),
        mode_weight,
        weight_first,
        weight_second,
    )
    out_real, out_imag, back_real, back_imag, grad_first, grad_second = results
    spec_out = jnp.stack(
        [jnp.stack([out_real, out_imag]), jnp.stack([back_real, back_imag])]
    ).reshape(2, 2, rows_total, KWD * channels)
    nat_cos, nat_sin = wave_table(
        jnp.arange(rows_total, dtype=jnp.int32), jnp.arange(rows_total, dtype=jnp.int32), rows_total
    )
    nat_coeffs = jnp.concatenate([nat_cos, nat_sin]).astype(jnp.bfloat16)
    product = jnp.einsum("ak,sqkc->saqc", nat_coeffs, spec_out, preferred_element_type=jnp.float32)
    upper = product[:, :rows_total]
    lower = product[:, rows_total:]
    inverse_rows = jnp.stack(
        [upper[:, :, 0] - lower[:, :, 1], lower[:, :, 0] + upper[:, :, 1]], axis=2
    ).astype(jnp.bfloat16)
    inverse_rows = inverse_rows.reshape(2, rows_total, 2, KWD, channels)
    returned = lax.all_to_all(
        lax.all_to_all(inverse_rows, "lat", split_axis=1, concat_axis=3, tiled=True),
        "lon",
        split_axis=1,
        concat_axis=3,
        tiled=True,
    )
    slot_index = jnp.arange(kept_total, dtype=jnp.int32)
    kw_of = (
        slot_index // KWD % lat_count * lon_count + slot_index // (lat_count * KWD)
    ) * KWD + slot_index % KWD
    inv_cos, inv_sin = wave_table(kw_of, jnp.arange(cols_total, dtype=jnp.int32), cols_total)
    plain = jnp.concatenate([inv_cos, -inv_sin]).astype(jnp.bfloat16)
    doubled = jnp.where(kw_of == 0, 1.0, 2.0).astype(jnp.float32)
    scaled = (plain.astype(jnp.float32) * jnp.concatenate([doubled, doubled])[:, None]).astype(
        jnp.bfloat16
    )
    returned_flat = returned.reshape(2, rows_each, 2 * kept_total, channels)
    filtered = jnp.einsum(
        "aw,rac->rwc", scaled, returned_flat[0], preferred_element_type=jnp.float32
    ).astype(jnp.bfloat16)
    backward = jnp.einsum(
        "aw,rac->rwc", plain, returned_flat[1], preferred_element_type=jnp.float32
    ).astype(jnp.bfloat16)
    spatial = lon_transpose(jnp.stack([filtered, backward]), 2, 1)
    mixed_field = (features.astype(jnp.float32) + spatial[0].astype(jnp.float32)).astype(
        jnp.bfloat16
    )
    feature_grad = (cotangent.astype(jnp.float32) + spatial[1].astype(jnp.float32)).astype(
        jnp.bfloat16
    )
    summed = lax.psum((grad_first, grad_second), ("lat", "lon"))
    factor = 1.0 / math.sqrt(rows_total * kept_total)
    return (mixed_field, feature_grad, summed[0] * factor, summed[1] * factor)


def solution(mesh):
    in_specs = (P("lat", "lon", None), P("lat", "lon", None), P(), P())
    out_specs = (P("lat", "lon", None), P("lat", "lon", None), P(), P())
    return jax.shard_map(shards, mesh=mesh, in_specs=in_specs, out_specs=out_specs, check_vma=False)
```

profile of v0, /device:TPU:2, one launch (start us, length us, event | category | flops | bytes accessed | tf_op | source)
XLA Modules:
  0.0 520.0 jit_solution(9959263662346330774)
XLA Ops:
  7.2 2.7 pad_maximum_fusion
  9.9 11.5 %all-to-all-start = ((bf16[2,32,16,768]{3,2,0,1:T(8,128)(2,1)}), bf16[2,32,16,768]{3,2,0,1:T(8,128)(2,1)S(1)}, u32[]{:S(2)}, u32[]{:S(2)}) async-start(bf16[2,32,16,768]{3,2,0,1:T(8,128)(2,1)} %pad_maximum_fusion), calls=%async_computation | async-start | bytes 3145728 | tf_op jit(solution)/shard_map/all_to_all | solution.py:90
  21.3 2.2 multiply_convert_fusion.7
  23.6 36.9 %all-to-all-done = bf16[2,32,16,768]{3,2,0,1:T(8,128)(2,1)S(1)} async-done(((bf16[2,32,16,768]{3,2,0,1:T(8,128)(2,1)}), bf16[2,32,16,768]{3,2,0,1:T(8,128)(2,1)S(1)}, u32[]{:S(2)}, u32[]{:S(2)}) %all-to-all-start) | async-done | bytes 1572896 | tf_op jit(solution)/shard_map/all_to_all | solution.py:90
  60.6 1.0 convolution_bitcast_fusion.2
  62.1 1.9 copy.79
  64.0 25.0 %all_to_all.84 = bf16[2,1,2,256,768]{4,0,2,1,3:T(2,128)(2,1)S(1)} all-to-all(bf16[2,1,2,256,768]{4,0,2,1,3:T(2,128)(2,1)S(1)} %copy.79), channel_id=1, replica_groups=mesh['lat'=8,'lon'=32] {'lat'}, dimensions={3} | all-to-all | bytes 3145728 | tf_op jit(solution)/shard_map/all_to_all | solution.py:120
  89.2 2.0 copy.81
  91.2 5.9 %all-to-all-start.2 = ((bf16[2,8,2,32,768]{4,1,2,0,3:T(8,128)(2,1)}), bf16[2,8,2,32,768]{4,1,2,0,3:T(8,128)(2,1)S(1)}, u32[]{:S(2)}, u32[]{:S(2)}) async-start(bf16[2,8,2,32,768]{4,1,2,0,3:T(8,128)(2,1)} %copy.81), calls=%async_computation.2 | async-start | bytes 3145728 | tf_op jit(solution)/shard_map/all_to_all | solution.py:119
  97.2 1.1 multiply_convert_fusion.9
  98.3 1.1 multiply_convert_fusion.12
  99.5 36.3 %all-to-all-done.2 = bf16[2,8,2,32,768]{4,1,2,0,3:T(8,128)(2,1)S(1)} async-done(((bf16[2,8,2,32,768]{4,1,2,0,3:T(8,128)(2,1)}), bf16[2,8,2,32,768]{4,1,2,0,3:T(8,128)(2,1)S(1)}, u32[]{:S(2)}, u32[]{:S(2)}) %all-to-all-start.2) | async-done | bytes 1572896 | tf_op jit(solution)/shard_map/all_to_all | solution.py:119
  135.7 1.0 convolution_bitcast_fusion.1
  136.8 0.4 fusion.4
  137.2 0.6 copy-done.2
  138.1 0.3 fusion.96
  138.5 0.5 multiply_convert_fusion.4
  138.9 0.5 copy-done.7
  139.7 0.3 fusion.76
  140.2 0.5 multiply_convert_fusion.3
  140.7 0.4 subtract_convert_fusion.1
  141.4 0.4 subtract_convert_fusion
  142.1 0.6 fusion.27
  142.9 0.6 fusion.28
  144.3 1.0 convolution_bitcast_fusion
  145.9 3.1 copy.98
  149.0 25.3 %all_to_all.85 = bf16[2,256,2,1,768]{4,0,3,2,1:T(2,128)(2,1)S(1)} all-to-all(bf16[2,256,2,1,768]{4,0,3,2,1:T(2,128)(2,1)} %copy.98), channel_id=1, replica_groups=mesh['lat'=8,'lon'=32] {'lat'}, dimensions={1} | all-to-all | bytes 3145728 | tf_op jit(solution)/shard_map/all_to_all | solution.py:174
  174.5 2.0 copy.100
  176.6 6.0 %all-to-all-start.4 = ((bf16[2,32,2,8,768]{4,3,2,0,1:T(8,128)(2,1)}), bf16[2,32,2,8,768]{4,3,2,0,1:T(8,128)(2,1)S(1)}, u32[]{:S(2)}, u32[]{:S(2)}) async-start(bf16[2,32,2,8,768]{4,3,2,0,1:T(8,128)(2,1)} %copy.100), calls=%async_computation.4 | async-start | bytes 3145728 | tf_op jit(solution)/shard_map/all_to_all | solution.py:173
  182.6 3.2 multiply_convert_fusion.6
  185.8 35.3 %all-to-all-done.4 = bf16[2,32,2,8,768]{4,3,2,0,1:T(8,128)(2,1)S(1)} async-done(((bf16[2,32,2,8,768]{4,3,2,0,1:T(8,128)(2,1)}), bf16[2,32,2,8,768]{4,3,2,0,1:T(8,128)(2,1)S(1)}, u32[]{:S(2)}, u32[]{:S(2)}) %all-to-all-start.4) | async-done | bytes 1572896 | tf_op jit(solution)/shard_map/all_to_all | solution.py:173
  221.3 0.8 copy-done.11
  222.2 0.6 fusion.18
  222.8 0.7 fusion.17
  223.7 3.0 copy.102
  226.6 5.8 %all-to-all-start.5 = ((bf16[2,1,512,768]{3,0,1,2:T(2,128)(2,1)}), bf16[2,1,512,768]{3,0,1,2:T(2,128)(2,1)S(1)}, u32[]{:S(2)}, u32[]{:S(2)}) async-start(bf16[2,1,512,768]{3,0,1,2:T(2,128)(2,1)} %copy.102), calls=%async_computation.5 | async-start | bytes 3145728 | tf_op jit(solution)/shard_map/all_to_all | solution.py:90
  232.5 1.3 fusion.127
  233.8 1.3 fusion.32
  235.7 0.9 pad_maximum_fusion.5
  237.7 0.9 pad_maximum_fusion.4
  238.6 264.8 %all-reduce.3.cloned.1.call-done = (f32[2,8,96,96]{3,2,1,0:T(8,128)}, f32[2,8,96,96]{3,2,1,0:T(8,128)}) async-done(((f32[2,8,96,96]{3,2,1,0:T(8,128)}, f32[2,8,96,96]{3,2,1,0:T(8,128)}), (f32[2,8,96,96]{3,2,1,0:T(8,128)}, f32[2,8,96,96]{3,2,1,0:T(8,128)})) %all-reduce.3.cloned.1.call-update) | async-done | bytes 1179664 | tf_op jit(solution)/shard_map/psum | solution.py:204
  503.4 2.2 broadcast_multiply_fusion
  505.6 0.9 broadcast_multiply_fusion.1
  506.5 2.2 fusion.123
  508.9 1.0 copy-done.8
  509.9 1.1 fusion.13
  511.1 1.0 copy-done.9
  512.1 1.1 fusion.14
  (59 shorter events, 6.1 us)
Async XLA Ops:
  9.9 50.6 %all-to-all-start = ((bf16[2,32,16,768]{3,2,0,1:T(8,128)(2,1)}), bf16[2,32,16,768]{3,2,0,1:T(8,128)(2,1)S(1)}, u32[]{:S(2)}, u32[]{:S(2)}) async-start(bf16[2,32,16,768]{3,2,0,1:T(8,128)(2,1)} %pad_maximum_fusion), calls=%async_computation | async-start | bytes 3145728 | tf_op jit(solution)/shard_map/all_to_all | solution.py:90
  91.2 44.5 %all-to-all-start.2 = ((bf16[2,8,2,32,768]{4,1,2,0,3:T(8,128)(2,1)}), bf16[2,8,2,32,768]{4,1,2,0,3:T(8,128)(2,1)S(1)}, u32[]{:S(2)}, u32[]{:S(2)}) async-start(bf16[2,8,2,32,768]{4,1,2,0,3:T(8,128)(2,1)} %copy.81), calls=%async_computation.2 | async-start | bytes 3145728 | tf_op jit(solution)/shard_map/all_to_all | solution.py:119
  136.8 1.0 copy-start.2
  138.4 1.0 copy-start.7
  141.1 1.8 copy-start.3
  141.8 0.9 copy-start.5
  143.5 0.8 copy-start
  176.6 44.5 %all-to-all-start.4 = ((bf16[2,32,2,8,768]{4,3,2,0,1:T(8,128)(2,1)}), bf16[2,32,2,8,768]{4,3,2,0,1:T(8,128)(2,1)S(1)}, u32[]{:S(2)}, u32[]{:S(2)}) async-start(bf16[2,32,2,8,768]{4,3,2,0,1:T(8,128)(2,1)} %copy.100), calls=%async_computation.4 | async-start | bytes 3145728 | tf_op jit(solution)/shard_map/all_to_all | solution.py:173
  221.2 1.0 copy-start.11
  221.2 1.0 copy-start.12
  226.6 279.9 %all-to-all-start.5 = ((bf16[2,1,512,768]{3,0,1,2:T(2,128)(2,1)}), bf16[2,1,512,768]{3,0,1,2:T(2,128)(2,1)S(1)}, u32[]{:S(2)}, u32[]{:S(2)}) async-start(bf16[2,1,512,768]{3,0,1,2:T(2,128)(2,1)} %copy.102), calls=%async_computation.5 | async-start | bytes 3145728 | tf_op jit(solution)/shard_map/all_to_all | solution.py:90
  232.4 271.0 %all-reduce.3.cloned.1.call-start = ((), (), s32[]{:S(2)}) async-start(), calls=%async_computation.6 | async-start | bytes 3145728 | tf_op jit(solution)/shard_map/psum | solution.py:204
  232.5 2.6 copy-start.6
  233.8 1.6 copy-start.4
  235.7 1.2 copy-start.1
  503.4 2.2 copy-start.10
  508.8 1.1 copy-start.8
  511.0 1.1 copy-start.9
Sparse Core Ops, SparseCore 0:
  239.4 263.9 all-reduce.2
where the time goes:
time: 521 us; the launch traced here: 520 us
  waiting for transfers between devices  373 us (72%)
  blocking collectives  50.3 us (10%)
  starting transfers between devices  29.2 us (6%)
  local copies, waits for them, and re-layouts  19.4 us (4%)
  other arithmetic  19 us (4%)
  between operations  14.6 us (3%)
  matrix products  14.2 us (3%)
    psum x1, waiting for transfers between devices, shards(): summed = lax.psum((grad_first, grad_second), ('lat', 'lon'))  265 us
    all_to_all x2, waiting for transfers between devices, lon_transpose(): lax.all_to_all(source, 'lon', split_axis=split_dim, concat_axis=concat_di...  36.9 us
    all_to_all x1, waiting for transfers between devices, shards(): lax.all_to_all(lax.all_to_all(spectral_rows, 'lat', split_axis=3, concat_...  36.3 us
    all_to_all x1, waiting for transfers between devices, shards(): lax.all_to_all(lax.all_to_all(inverse_rows, 'lat', split_axis=1, concat_a...  35.3 us
    all_to_all x1, blocking collectives, shards(): lax.all_to_all(inverse_rows, 'lat', split_axis=1, concat_axis=3, tiled=True)  25.3 us
    all_to_all x1, blocking collectives, shards(): lax.all_to_all(spectral_rows, 'lat', split_axis=3, concat_axis=1, tiled=T...  25 us
    all_to_all x2, starting transfers between devices, lon_transpose(): lax.all_to_all(source, 'lon', split_axis=split_dim, concat_axis=concat_di...  17.3 us
  transfers between devices with their start and end apart: 5, of which 4 were waited for; matrix products, arithmetic and copies ran while one was open for 3% of the time, Pallas kernels for 0%

commit v1 on v0

--- a/solution.py
+++ b/solution.py
@@ -201,7 +201,7 @@
     feature_grad = (cotangent.astype(jnp.float32) + spatial[1].astype(jnp.float32)).astype(
         jnp.bfloat16
     )
-    summed = lax.psum((grad_first, grad_second), ("lat", "lon"))
+    summed = lax.psum(lax.psum((grad_first, grad_second), "lon"), "lat")
     factor = 1.0 / math.sqrt(rows_total * kept_total)
     return (mixed_field, feature_grad, summed[0] * factor, summed[1] * factor)
 

time: 521 us -> 484 us (0.929)
  waiting for transfers between devices: 373 us -> 331 us
    psum x1 -> x2, waiting for transfers between devices: 265 us -> 227 us  [shards(): summed = lax.psum(lax.psum((grad_first, grad_second), 'lon'), 'lat')]
  transfers between devices with their start and end apart: 5 -> 6, of which waited for: 4 -> 5; matrix products, arithmetic and copies ran while one was open for 3% -> 4% of each run, Pallas kernels for 0% -> 0%
where the time goes in v1:
time: 484 us; the launch traced here: 480 us
  waiting for transfers between devices  331 us (68%)
  blocking collectives  50.3 us (10%)
  starting transfers between devices  29.4 us (6%)
  other arithmetic  20.1 us (4%)
  local copies, waits for them, and re-layouts  19.5 us (4%)
  matrix products  15.4 us (3%)
  between operations  14.6 us (3%)
    psum x2, waiting for transfers between devices, shards(): summed = lax.psum(lax.psum((grad_first, grad_second), 'lon'), 'lat')  227 us
    all_to_all x2, waiting for transfers between devices, lon_transpose(): lax.all_to_all(source, 'lon', split_axis=split_dim, concat_axis=concat_di...  36.9 us
    all_to_all x1, waiting for transfers between devices, shards(): lax.all_to_all(lax.all_to_all(spectral_rows, 'lat', split_axis=3, concat_...  36.3 us
    all_to_all x1, waiting for transfers between devices, shards(): lax.all_to_all(lax.all_to_all(inverse_rows, 'lat', split_axis=1, concat_a...  30.7 us
    all_to_all x1, blocking collectives, shards(): lax.all_to_all(inverse_rows, 'lat', split_axis=1, concat_axis=3, tiled=True)  25.3 us
    all_to_all x1, blocking collectives, shards(): lax.all_to_all(spectral_rows, 'lat', split_axis=3, concat_axis=1, tiled=T...  25 us
    all_to_all x2, starting transfers between devices, lon_transpose(): lax.all_to_all(source, 'lon', split_axis=split_dim, concat_axis=concat_di...  17.4 us
  transfers between devices with their start and end apart: 6, of which 5 were waited for; matrix products, arithmetic and copies ran while one was open for 4% of the time, Pallas kernels for 0%

profile of v1, /device:TPU:2, one launch (start us, length us, event | category | flops | bytes accessed | tf_op | source)
XLA Modules:
  0.0 480.4 jit_solution(10922052617766213827)
XLA Ops:
  7.2 2.7 pad_maximum_fusion
  9.9 11.5 %all-to-all-start = ((bf16[2,32,16,768]{3,2,0,1:T(8,128)(2,1)}), bf16[2,32,16,768]{3,2,0,1:T(8,128)(2,1)S(1)}, u32[]{:S(2)}, u32[]{:S(2)}) async-start(bf16[2,32,16,768]{3,2,0,1:T(8,128)(2,1)} %pad_maximum_fusion), calls=%async_computation | async-start | bytes 3145728 | tf_op jit(solution)/shard_map/all_to_all | solution.py:90
  21.4 2.2 multiply_convert_fusion.7
  23.6 36.9 %all-to-all-done = bf16[2,32,16,768]{3,2,0,1:T(8,128)(2,1)S(1)} async-done(((bf16[2,32,16,768]{3,2,0,1:T(8,128)(2,1)}), bf16[2,32,16,768]{3,2,0,1:T(8,128)(2,1)S(1)}, u32[]{:S(2)}, u32[]{:S(2)}) %all-to-all-start) | async-done | bytes 1572896 | tf_op jit(solution)/shard_map/all_to_all | solution.py:90
  60.6 1.0 convolution_bitcast_fusion.2
  62.1 1.9 copy.79
  64.0 25.0 %all_to_all.84 = bf16[2,1,2,256,768]{4,0,2,1,3:T(2,128)(2,1)S(1)} all-to-all(bf16[2,1,2,256,768]{4,0,2,1,3:T(2,128)(2,1)S(1)} %copy.79), channel_id=1, replica_groups=mesh['lat'=8,'lon'=32] {'lat'}, dimensions={3} | all-to-all | bytes 3145728 | tf_op jit(solution)/shard_map/all_to_all | solution.py:120
  89.2 2.1 copy.81
  91.3 5.9 %all-to-all-start.2 = ((bf16[2,8,2,32,768]{4,1,2,0,3:T(8,128)(2,1)}), bf16[2,8,2,32,768]{4,1,2,0,3:T(8,128)(2,1)S(1)}, u32[]{:S(2)}, u32[]{:S(2)}) async-start(bf16[2,8,2,32,768]{4,1,2,0,3:T(8,128)(2,1)} %copy.81), calls=%async_computation.2 | async-start | bytes 3145728 | tf_op jit(solution)/shard_map/all_to_all | solution.py:119
  97.2 1.1 multiply_convert_fusion.9
  98.4 1.1 multiply_convert_fusion.12
  99.5 36.3 %all-to-all-done.2 = bf16[2,8,2,32,768]{4,1,2,0,3:T(8,128)(2,1)S(1)} async-done(((bf16[2,8,2,32,768]{4,1,2,0,3:T(8,128)(2,1)}), bf16[2,8,2,32,768]{4,1,2,0,3:T(8,128)(2,1)S(1)}, u32[]{:S(2)}, u32[]{:S(2)}) %all-to-all-start.2) | async-done | bytes 1572896 | tf_op jit(solution)/shard_map/all_to_all | solution.py:119
  135.8 1.0 convolution_bitcast_fusion.1
  137.3 0.6 copy-done.2
  138.5 0.5 multiply_convert_fusion.4
  139.0 0.5 copy-done.7
  140.2 0.5 multiply_convert_fusion.3
  140.7 0.4 subtract_convert_fusion.1
  141.4 0.4 subtract_convert_fusion
  142.1 0.6 fusion.27
  143.0 0.6 fusion.28
  144.4 1.0 convolution_bitcast_fusion
  145.9 3.1 copy.98
  149.1 25.3 %all_to_all.85 = bf16[2,256,2,1,768]{4,0,3,2,1:T(2,128)(2,1)S(1)} all-to-all(bf16[2,256,2,1,768]{4,0,3,2,1:T(2,128)(2,1)} %copy.98), channel_id=1, replica_groups=mesh['lat'=8,'lon'=32] {'lat'}, dimensions={1} | all-to-all | bytes 3145728 | tf_op jit(solution)/shard_map/all_to_all | solution.py:174
  174.6 2.1 copy.100
  176.6 6.0 %all-to-all-start.4 = ((bf16[2,32,2,8,768]{4,3,2,0,1:T(8,128)(2,1)}), bf16[2,32,2,8,768]{4,3,2,0,1:T(8,128)(2,1)S(1)}, u32[]{:S(2)}, u32[]{:S(2)}) async-start(bf16[2,32,2,8,768]{4,3,2,0,1:T(8,128)(2,1)} %copy.100), calls=%async_computation.4 | async-start | bytes 3145728 | tf_op jit(solution)/shard_map/all_to_all | solution.py:173
  182.7 3.2 multiply_convert_fusion.6
  185.9 1.2 fusion.127
  187.2 1.0 fusion.32
  188.4 1.0 fusion.31
  189.5 1.0 fusion.125
  190.5 30.7 %all-to-all-done.4 = bf16[2,32,2,8,768]{4,3,2,0,1:T(8,128)(2,1)S(1)} async-done(((bf16[2,32,2,8,768]{4,3,2,0,1:T(8,128)(2,1)}), bf16[2,32,2,8,768]{4,3,2,0,1:T(8,128)(2,1)S(1)}, u32[]{:S(2)}, u32[]{:S(2)}) %all-to-all-start.4) | async-done | bytes 1572896 | tf_op jit(solution)/shard_map/all_to_all | solution.py:173
  221.4 0.8 copy-done.13
  222.3 0.6 fusion.18
  222.9 0.7 fusion.17
  223.7 3.0 copy.102
  226.7 5.9 %all-to-all-start.5 = ((bf16[2,1,512,768]{3,0,1,2:T(2,128)(2,1)}), bf16[2,1,512,768]{3,0,1,2:T(2,128)(2,1)S(1)}, u32[]{:S(2)}, u32[]{:S(2)}) async-start(bf16[2,1,512,768]{3,0,1,2:T(2,128)(2,1)} %copy.102), calls=%async_computation.5 | async-start | bytes 3145728 | tf_op jit(solution)/shard_map/all_to_all | solution.py:90
  232.7 2.0 pad_maximum_fusion.5
  235.5 0.9 pad_maximum_fusion.4
  236.5 160.6 %all-reduce.5.cloned.1.call-done = (f32[2,8,96,96]{3,2,1,0:T(8,128)}, f32[2,8,96,96]{3,2,1,0:T(8,128)}) async-done(((f32[2,8,96,96]{3,2,1,0:T(8,128)}, f32[2,8,96,96]{3,2,1,0:T(8,128)}), (f32[2,8,96,96]{3,2,1,0:T(8,128)}, f32[2,8,96,96]{3,2,1,0:T(8,128)})) %all-reduce.5.cloned.1.call-update) | async-done | bytes 1179664 | tf_op jit(solution)/shard_map/psum | solution.py:204
  397.1 66.8 %all-reduce.7.cloned.1.call-done = (f32[2,8,96,96]{3,2,1,0:T(8,128)}, f32[2,8,96,96]{3,2,1,0:T(8,128)}) async-done(((f32[2,8,96,96]{3,2,1,0:T(8,128)}, f32[2,8,96,96]{3,2,1,0:T(8,128)}), (f32[2,8,96,96]{3,2,1,0:T(8,128)}, f32[2,8,96,96]{3,2,1,0:T(8,128)})) %all-reduce.7.cloned.1.call-update) | async-done | bytes 1179664 | tf_op jit(solution)/shard_map/psum | solution.py:204
  463.9 2.2 broadcast_multiply_fusion
  466.0 0.9 broadcast_multiply_fusion.1
  467.0 2.2 fusion.123
  469.3 1.0 copy-done.8
  470.3 1.1 fusion.13
  471.5 1.0 copy-done.9
  472.5 1.1 fusion.14
  (66 shorter events, 6.7 us)
Async XLA Ops:
  9.9 50.6 %all-to-all-start = ((bf16[2,32,16,768]{3,2,0,1:T(8,128)(2,1)}), bf16[2,32,16,768]{3,2,0,1:T(8,128)(2,1)S(1)}, u32[]{:S(2)}, u32[]{:S(2)}) async-start(bf16[2,32,16,768]{3,2,0,1:T(8,128)(2,1)} %pad_maximum_fusion), calls=%async_computation | async-start | bytes 3145728 | tf_op jit(solution)/shard_map/all_to_all | solution.py:90
  91.3 44.5 %all-to-all-start.2 = ((bf16[2,8,2,32,768]{4,1,2,0,3:T(8,128)(2,1)}), bf16[2,8,2,32,768]{4,1,2,0,3:T(8,128)(2,1)S(1)}, u32[]{:S(2)}, u32[]{:S(2)}) async-start(bf16[2,8,2,32,768]{4,1,2,0,3:T(8,128)(2,1)} %copy.81), calls=%async_computation.2 | async-start | bytes 3145728 | tf_op jit(solution)/shard_map/all_to_all | solution.py:119
  136.8 1.0 copy-start.2
  138.4 1.0 copy-start.7
  141.1 1.8 copy-start.3
  141.8 0.9 copy-start.5
  143.6 0.8 copy-start
  176.6 44.5 %all-to-all-start.4 = ((bf16[2,32,2,8,768]{4,3,2,0,1:T(8,128)(2,1)}), bf16[2,32,2,8,768]{4,3,2,0,1:T(8,128)(2,1)S(1)}, u32[]{:S(2)}, u32[]{:S(2)}) async-start(bf16[2,32,2,8,768]{4,3,2,0,1:T(8,128)(2,1)} %copy.100), calls=%async_computation.4 | async-start | bytes 3145728 | tf_op jit(solution)/shard_map/all_to_all | solution.py:173
  182.6 4.5 copy-start.6
  187.1 1.3 copy-start.4
  221.3 1.0 copy-start.13
  221.3 1.0 copy-start.14
  226.7 6.0 %copy-start.10 = (f32[1,8,96,96]{3,2,1,0:T(8,128)S(1)}, f32[1,8,96,96]{3,2,1,0:T(8,128)}, u32[]{:S(2)}) copy-start(f32[1,8,96,96]{3,2,1,0:T(8,128)} %fusion.32) | copy-start | bytes 884740
  226.7 240.2 %all-to-all-start.5 = ((bf16[2,1,512,768]{3,0,1,2:T(2,128)(2,1)}), bf16[2,1,512,768]{3,0,1,2:T(2,128)(2,1)S(1)}, u32[]{:S(2)}, u32[]{:S(2)}) async-start(bf16[2,1,512,768]{3,0,1,2:T(2,128)(2,1)} %copy.102), calls=%async_computation.5 | async-start | bytes 3145728 | tf_op jit(solution)/shard_map/all_to_all | solution.py:90
  232.6 2.1 copy-start.1
  232.6 164.4 %all-reduce.5.cloned.1.call-start = ((), (), s32[]{:S(2)}) async-start(), calls=%async_computation.6 | async-start | bytes 3145728 | tf_op jit(solution)/shard_map/psum | solution.py:204
  232.7 2.0 copy-start.11
  236.5 227.4 %all-reduce.7.cloned.1.call-start = ((), (), s32[]{:S(2)}) async-start(), calls=%async_computation.7 | async-start | bytes 3145728 | tf_op jit(solution)/shard_map/psum | solution.py:204
  463.9 2.2 copy-start.12
  469.2 1.1 copy-start.8
  471.4 1.1 copy-start.9
Sparse Core Ops, SparseCore 0:
  237.5 159.5 all-reduce.4
  399.7 64.1 all-reduce.6
